TPU v7x, 256 devices: a whole 4x4x8 slice. The times are simulated.
256 devices in a mesh: rep: 8 (over z), exp: 32 (over x, y, core).
Axes of the slice: x: 4, y: 4, z: 8, core: 2. Of those that a mesh axis runs over, the one named last changes fastest.
Arguments:
- tokens: bfloat16 [4096, 4096], P(('rep', 'exp')), may hold values from -6 to 6
- routed_experts: int32 [4096, 8], P(('rep', 'exp')), may hold values from 0 to 63, all different within a row; in each aligned block of 16 rows (0 to 15, 16 to 31, ...) at most 3 rows name the same one
- route_weights: float32 [4096, 8], P(('rep', 'exp')), may hold values from 0.02 to 0.5
- gate_weight: bfloat16 [64, 1536, 4096], P('exp', 'rep'), may hold values from -0.09375 to 0.09375
- up_weight: bfloat16 [64, 1536, 4096], P('exp', 'rep'), may hold values from -0.09375 to 0.09375
- down_weight: bfloat16 [64, 1536, 4096], P('exp', 'rep'), may hold values from -0.15625 to 0.15625
Outputs:
- layer_output: bfloat16 [4096, 4096], P(('rep', 'exp'))
Inputs may be any that keep to these rules, and one draw needn't show every extreme that they name: `routed_experts`: each token names 8 different experts. Among the 16 tokens of one device (aligned blocks of rows), no expert is named more than 3 times, a bound that some block reaches.
All inputs are finite; a program needn't handle non-finite values.
Results may differ from a plain program's by a relative error of at most 0.01.
Values may be sent and summed in bfloat16 or wider, within the bound.
A program may use at most 128 MiB of HBM per device.

v0:
```python
import jax
import jax.numpy as jnp
from jax import lax
from jax.sharding import PartitionSpec as P


def slot_table(experts, expert_count, capacity):
    blocks = experts.shape[0]
    flattened = experts.reshape(blocks, -1)
    onehot = (
        flattened[:, :, None] == jnp.arange(expert_count, dtype=jnp.int32)[None, None, :]
    ).astype(jnp.int32)
    before = jnp.cumsum(onehot, axis=1) - onehot
    position = jnp.sum(before * onehot, axis=2)
    return flattened * capacity + position


def token_picks(slots, top_count, slot_count):
    blocks = slots.shape[0]
    grouped = slots.reshape(blocks, 1, -1, top_count)
    return jnp.any(grouped == jnp.arange(slot_count, dtype=jnp.int32)[None, :, None, None], axis=3)


def routing_column(route_weights, routed_experts):
    as_float = routed_experts.astype(jnp.float32)
    weights_all, experts_all = (
        lax.all_gather(route_weights, "rep", axis=0, tiled=True),
        lax.all_gather(as_float, "rep", axis=0, tiled=True),
    )
    return (weights_all, experts_all.astype(jnp.int32))


def on_device(tokens, routed_experts, route_weights, gate_weight, up_weight, down_weight):
    replicas = lax.axis_size("rep")
    owners = lax.axis_size("exp")
    token_rows, model_width = tokens.shape
    top_count = routed_experts.shape[1]
    local_experts = gate_weight.shape[0]
    expert_count = local_experts * owners
    capacity = max(2, 3 * token_rows * top_count // (2 * expert_count))
    slot_count = expert_count * capacity
    own_slots = slot_table(routed_experts[None], expert_count, capacity)
    column = None
    column_slots = None
    selected = token_picks(own_slots, top_count, slot_count)[0].astype(jnp.bfloat16)
    buffer = jnp.dot(selected, tokens, preferred_element_type=jnp.float32).astype(jnp.bfloat16)
    buffer = buffer.reshape(owners, local_experts, capacity, model_width)
    arrived = lax.all_to_all(buffer, "exp", split_axis=0, concat_axis=2, tiled=True)
    rows_now = lax.all_gather(arrived, "rep", axis=2, tiled=True)[0]
    gate_value = jnp.einsum(
        "emd,efd->emf", rows_now, gate_weight, preferred_element_type=jnp.float32
    )
    up_value = jnp.einsum("emd,efd->emf", rows_now, up_weight, preferred_element_type=jnp.float32)
    hidden = (jax.nn.silu(gate_value) * up_value).astype(jnp.bfloat16)
    outcome = jnp.einsum("emf,efd->emd", hidden, down_weight, preferred_element_type=jnp.float32)
    outcome = lax.optimization_barrier(outcome.astype(jnp.bfloat16))
    outcomes = outcome[None]
    outcomes = outcomes.reshape(local_experts, replicas, owners, capacity, model_width)
    column = routing_column(route_weights, routed_experts)
    column_slots = slot_table(
        column[1].reshape(replicas, token_rows, top_count), expert_count, capacity
    )
    returned = lax.all_to_all(outcomes, "exp", split_axis=2, concat_axis=0, tiled=True)
    returned = returned.reshape(expert_count, replicas, capacity, model_width)
    expert_index = column_slots // capacity
    place_index = column_slots % capacity
    replica_index = jnp.broadcast_to(
        jnp.arange(replicas, dtype=jnp.int32)[:, None], column_slots.shape
    )
    picked = returned[expert_index, replica_index, place_index].astype(jnp.float32)
    column_weights = column[0].reshape(replicas, token_rows, top_count)
    weighted = jnp.sum(
        picked.reshape(replicas, token_rows, top_count, model_width)
        * column_weights[:, :, :, None],
        axis=2,
    )
    summed = lax.psum_scatter(weighted, "rep", scatter_dimension=0, tiled=True)
    return summed.reshape(token_rows, model_width).astype(jnp.bfloat16)


def solution(mesh):
    placed = (
        P(("rep", "exp"), None),
        P(("rep", "exp"), None),
        P(("rep", "exp"), None),
        P("exp", "rep", None),
        P("exp", "rep", None),
        P("exp", "rep", None),
    )
    return jax.shard_map(
        on_device, mesh=mesh, in_specs=placed, out_specs=P(("rep", "exp"), None), check_vma=False
    )
```

profile of v0, /device:TPU:2, one launch (start us, length us, event | category | flops | bytes accessed | tf_op | source)
XLA Modules:
  0.0 557.9 jit_solution(14770991850050571050)
XLA Ops:
  6.5 0.9 copy.34
  7.4 0.1 eq.65
  7.5 0.1 fusion.25
  7.6 0.2 reduce_window_sum.22
  7.8 0.2 select_reduce_fusion.1
  8.0 0.1 reduce_sum.32
  8.1 0.1 fusion.24
  8.2 2.7 convolution_convert_fusion.1
  10.9 4.1 reshape.225
  15.0 3.6 copy.36
  18.6 28.4 %all_to_all.33 = bf16[32,2,3,4096]{3,1,2,0:T(2,128)(2,1)S(1)} all-to-all(bf16[32,2,3,4096]{3,1,2,0:T(2,128)(2,1)S(1)} %copy.36), channel_id=1, replica_groups=mesh['rep'=8,'exp'=32] {'exp'}, dimensions={0} | all-to-all | bytes 3145728 | tf_op jit(solution)/shard_map/all_to_all | solution.py:48
  47.0 2.1 copy.37
  49.1 134.3 %all-gather.4.cloned.1.call-done = bf16[1,2,768,4096]{3,2,1,0:T(8,128)(2,1)} async-done(((bf16[1,2,96,4096]{3,2,1,0:T(8,128)(2,1)}), bf16[1,2,768,4096]{3,2,1,0:T(8,128)(2,1)}) %all-gather.4.cloned.1.call-update) | async-done | bytes 12582928 | tf_op jit(solution)/shard_map/all_gather | solution.py:49
  183.4 10.9 %fusion.3 = f32[2,768,192]{1,2,0:T(8,128)} fusion(bf16[2,192,4096]{2,1,0:T(8,128)(2,1)} %param.9, bf16[1,2,768,4096]{3,2,1,0:T(8,128)(2,1)} %all-gather.4.cloned.1.call-done), kind=kOutput, calls=%fused_computation.5 | convolution fusion | flops 2415919104 | bytes 16908288 | tf_op jit(solution)/shard_map/emd,efd->emf/dot_general | solution.py:50
  194.3 15.9 %convolution_convert_fusion = bf16[2,768,4096]{2,1,0:T(8,128)(2,1)} fusion(bf16[2,192,4096]{2,1,0:T(8,128)(2,1)S(1)} %copy-done, bf16[2,192,4096]{2,1,0:T(8,128)(2,1)} %param.10, bf16[1,2,768,4096]{3,2,1,0:T(8,128)(2,1)} %all-gather.4.cloned.1.call-done, f32[2,768,192]{1,2,0:T(8,128)} %fusion.3), kind=kOutput, calls=%fused_computation.7 | convolution fusion | flops 4839899136 | bytes 32636928 | tf_op jit(solution)/shard_map/emf,efd->emd/dot_general | solution.py:55
  210.2 21.2 %copy.38 = bf16[2,768,4096]{2,0,1:T(2,128)(2,1)S(1)} copy(bf16[2,768,4096]{2,1,0:T(8,128)(2,1)} %convolution_convert_fusion) | data formatting | bytes 25165824 | tf_op jit(solution)/shard_map/optimization_barrier | solution.py:56
  231.5 11.5 %copy.39 = bf16[2,8,32,3,4096]{4,0,3,1,2:T(2,128)(2,1)} copy(bf16[2,8,32,3,4096]{4,0,3,2,1:T(2,128)(2,1)S(1)} %bitcast.42) | data formatting | bytes 25165824 | tf_op jit(solution)/shard_map/reshape;broadcast_in_dim | solution.py:58
  243.0 7.6 %all-to-all-start.1 = ((bf16[2,8,32,3,4096]{4,0,3,1,2:T(2,128)(2,1)}), bf16[2,8,32,3,4096]{4,0,3,1,2:T(2,128)(2,1)}, u32[]{:S(2)}, u32[]{:S(2)}) async-start(bf16[2,8,32,3,4096]{4,0,3,1,2:T(2,128)(2,1)} %copy.39), calls=%async_computation.1 | async-start | bytes 25165824 | tf_op jit(solution)/shard_map/all_to_all | solution.py:63
  250.6 0.0 reduce-scatter.2.cloned.1.call-start
  250.7 24.9 %all-gather = f32[8,16,8]{1,2,0:T(8,128)S(1)} all-gather(f32[1,16,8]{1,2,0:T(8,128)S(1)} %convert_bitcast_fusion.1), channel_id=1, replica_groups=mesh['rep'=8,'exp'=32] {'rep'}, dimensions={0}, use_global_device_ids=true | all-gather | bytes 4608 | tf_op jit(solution)/shard_map/all_gather | solution.py:28
  275.6 0.1 copy.46
  275.7 2.5 select_reduce_fusion
  278.3 0.1 copy.41
  278.4 0.1 mul.56
  278.5 24.7 %all-gather.1 = f32[8,16,8]{1,2,0:T(8,128)S(1)} all-gather(f32[1,16,8]{1,2,0:T(8,128)S(1)} %bitcast.45), channel_id=1, replica_groups=mesh['rep'=8,'exp'=32] {'rep'}, dimensions={0}, use_global_device_ids=true | all-gather | bytes 4608 | tf_op jit(solution)/shard_map/all_gather | solution.py:27
  303.1 0.1 copy.45
  303.3 115.4 %all-to-all-done.1 = bf16[2,8,32,3,4096]{4,0,3,1,2:T(2,128)(2,1)} async-done(((bf16[2,8,32,3,4096]{4,0,3,1,2:T(2,128)(2,1)}), bf16[2,8,32,3,4096]{4,0,3,1,2:T(2,128)(2,1)}, u32[]{:S(2)}, u32[]{:S(2)}) %all-to-all-start.1) | async-done | bytes 12582944 | tf_op jit(solution)/shard_map/all_to_all | solution.py:63
  418.7 14.5 %copy.40 = bf16[32,2,8,1,3,4096]{5,2,4,1,0,3:T(8,128)(2,1)} copy(bf16[32,2,8,1,3,4096]{5,1,4,2,0,3:T(2,128)(2,1)} %bitcast.6) | data formatting | bytes 25165824 | tf_op jit(solution)/shard_map/all_to_all | solution.py:63
  433.2 34.4 %gather_fusion = bf16[1024,4096]{1,0:T(8,128)(2,1)} fusion(bf16[64,8,3,4096]{3,1,2,0:T(8,128)(2,1)} %bitcast.41, s32[1024]{0:T(1024)S(1)} %fusion.30), kind=kCustom, calls=%fused_computation | custom fusion | bytes 16789504 | tf_op jit(solution)/shard_map/gather | solution.py:70
  467.6 12.9 %fusion = f32[8,16,4096]{2,1,0:T(8,128)} fusion(f32[8,16,8]{2,1,0:T(8,128)S(1)} %copy.45, bf16[1024,4096]{1,0:T(8,128)(2,1)} %gather_fusion), kind=kLoop, calls=%fused_computation.2 | loop fusion | flops 12058624 | bytes 10489856 | tf_op jit(solution)/shard_map/reduce_sum | solution.py:72
  480.6 68.8 %reduce-scatter.2.cloned.1.call-done = f32[1,16,4096]{2,1,0:T(8,128)} async-done(((f32[8,16,4096]{2,1,0:T(8,128)}), f32[1,16,4096]{2,1,0:T(8,128)}) %reduce-scatter.2.cloned.1.call-update) | async-done | bytes 262160 | tf_op jit(solution)/shard_map/reduce_scatter | solution.py:77
  549.4 1.6 convert_bitcast_fusion
  (17 shorter events, 0.2 us)
Async XLA Ops:
  6.5 187.8 %copy-start = (bf16[2,192,4096]{2,1,0:T(8,128)(2,1)S(1)}, bf16[2,192,4096]{2,1,0:T(8,128)(2,1)}, u32[]{:S(2)}) copy-start(bf16[2,192,4096]{2,1,0:T(8,128)(2,1)} %param.11) | copy-start | bytes 9437188
  6.5 176.9 %all-gather.4.cloned.1.call-start = ((), (), s32[]{:S(2)}) async-start(), calls=%async_computation.3 | async-start | bytes 14155776 | tf_op jit(solution)/shard_map/all_gather | solution.py:49
  243.0 7.7 %copy-start.2 = (s32[16,8]{0,1:T(8,128)S(1)}, s32[16,8]{0,1:T(8,128)}, u32[]{:S(2)}) copy-start(s32[16,8]{0,1:T(8,128)} %param.7) | copy-start | bytes 1540
  243.0 35.5 %copy-start.3 = (f32[16,8]{0,1:T(8,128)S(1)}, f32[16,8]{0,1:T(8,128)}, u32[]{:S(2)}) copy-start(f32[16,8]{0,1:T(8,128)} %param.8) | copy-start | bytes 1540
  243.0 175.7 %all-to-all-start.1 = ((bf16[2,8,32,3,4096]{4,0,3,1,2:T(2,128)(2,1)}), bf16[2,8,32,3,4096]{4,0,3,1,2:T(2,128)(2,1)}, u32[]{:S(2)}, u32[]{:S(2)}) async-start(bf16[2,8,32,3,4096]{4,0,3,1,2:T(2,128)(2,1)} %copy.39), calls=%async_computation.1 | async-start | bytes 25165824 | tf_op jit(solution)/shard_map/all_to_all | solution.py:63
  250.6 298.8 %reduce-scatter.2.cloned.1.call-start = ((), (), s32[]{:S(2)}) async-start(), calls=%async_computation.4 | async-start | bytes 2359296 | tf_op jit(solution)/shard_map/reduce_scatter | solution.py:77
  467.6 83.4 %copy-start.1 = (bf16[2,192,4096]{2,1,0:T(8,128)(2,1)S(1)}, bf16[2,192,4096]{2,1,0:T(8,128)(2,1)}, u32[]{:S(2)}) copy-start(bf16[2,192,4096]{2,1,0:T(8,128)(2,1)} %param.11) | copy-start | bytes 9437188
Sparse Core Ops, SparseCore 0:
  49.3 134.1 all-gather.3
  480.7 68.6 reduce-scatter.1
where the time goes:
time: 559 us; the launch traced here: 558 us
  waiting for transfers between devices  319 us (57%)
  local copies, waits for them, and re-layouts  93 us (17%)
  blocking collectives  78 us (14%)
  matrix products  29.5 us (5%)
  other arithmetic  17.7 us (3%)
  between operations  13.5 us (2%)
  starting transfers between devices  7.64 us (1%)
    all_gather x1, waiting for transfers between devices, on_device(): rows_now = lax.all_gather(arrived, 'rep', axis=2, tiled=True)[0]  134 us
    all_to_all x1, waiting for transfers between devices, on_device(): lax.all_to_all(outcomes, 'exp', split_axis=2, concat_axis=0, tiled=True)  115 us
    reduce_scatter x1, waiting for transfers between devices, on_device(): summed = lax.psum_scatter(weighted, 'rep', scatter_dimension=0, tiled=True)  68.8 us
    gather x1, local copies, waits for them, and re-layouts, on_device(): returned[expert_index, replica_index, place_index].astype(jnp.float32)  34.4 us
    all_to_all x1, blocking collectives, on_device(): lax.all_to_all(buffer, 'exp', split_axis=0, concat_axis=2, tiled=True)  28.4 us
    all_gather x1, blocking collectives, routing_column(): lax.all_gather(as_float, 'rep', axis=0, tiled=True)  24.9 us
    all_gather x1, blocking collectives, routing_column(): lax.all_gather(route_weights, 'rep', axis=0, tiled=True)  24.7 us
    optimization_barrier x1, local copies, waits for them, and re-layouts, on_device(): outcome = lax.optimization_barrier(outcome.astype(jnp.bfloat16))  21.2 us
  transfers between devices with their start and end apart: 3, of which 3 were waited for; matrix products, arithmetic and copies ran while one was open for 1% of the time, Pallas kernels for 0%

commit v1 on v0

--- a/solution.py
+++ b/solution.py
@@ -46,7 +46,9 @@
     buffer = jnp.dot(selected, tokens, preferred_element_type=jnp.float32).astype(jnp.bfloat16)
     buffer = buffer.reshape(owners, local_experts, capacity, model_width)
     arrived = lax.all_to_all(buffer, "exp", split_axis=0, concat_axis=2, tiled=True)
-    rows_now = lax.all_gather(arrived, "rep", axis=2, tiled=True)[0]
+    rows_now = jnp.concatenate(
+        lax.all_to_all(jnp.stack([arrived] * lax.axis_size("rep")), "rep", 0, 0), axis=2
+    )[0]
     gate_value = jnp.einsum(
         "emd,efd->emf", rows_now, gate_weight, preferred_element_type=jnp.float32
     )

time: 559 us -> 719 us (1.29)
  blocking collectives: 78 us -> 363 us
  waiting for transfers between devices: 319 us -> 182 us
  local copies, waits for them, and re-layouts: 93 us -> 106 us
    all_to_all x0 -> x1, blocking collectives: none -> 285 us  [on_device(): lax.all_to_all(jnp.stack([arrived] * lax.axis_size('rep')), 'rep', 0, 0)]
    all_gather x1 -> x0, waiting for transfers between devices: 134 us -> none  [on_device(): rows_now = lax.all_gather(arrived, 'rep', axis=2, tiled=True)[0]]
    another operation x0 -> x2, local copies, waits for them, and re-layouts: none -> 9.64 us  [on_device(): jnp.stack([arrived] * lax.axis_size('rep'))]
  transfers between devices with their start and end apart: 3 -> 2, of which waited for: 3 -> 2; matrix products, arithmetic and copies ran while one was open for 1% -> 0% of each run, Pallas kernels for 0% -> 0%
where the time goes in v1:
time: 719 us; the launch traced here: 718 us
  blocking collectives  363 us (50%)
  waiting for transfers between devices  182 us (25%)
  local copies, waits for them, and re-layouts  106 us (15%)
  matrix products  29.5 us (4%)
  other arithmetic  17.7 us (2%)
  between operations  13.5 us (2%)
    all_to_all x1, blocking collectives, on_device(): lax.all_to_all(jnp.stack([arrived] * lax.axis_size('rep')), 'rep', 0, 0)  285 us
    all_to_all x1, waiting for transfers between devices, on_device(): lax.all_to_all(outcomes, 'exp', split_axis=2, concat_axis=0, tiled=True)  114 us
    reduce_scatter x1, waiting for transfers between devices, on_device(): summed = lax.psum_scatter(weighted, 'rep', scatter_dimension=0, tiled=True)  68 us
    gather x1, local copies, waits for them, and re-layouts, on_device(): returned[expert_index, replica_index, place_index].astype(jnp.float32)  34.4 us
    all_to_all x1, blocking collectives, on_device(): lax.all_to_all(buffer, 'exp', split_axis=0, concat_axis=2, tiled=True)  28.4 us
    all_gather x1, blocking collectives, routing_column(): lax.all_gather(route_weights, 'rep', axis=0, tiled=True)  24.9 us
    all_gather x1, blocking collectives, routing_column(): lax.all_gather(as_float, 'rep', axis=0, tiled=True)  24.7 us
    optimization_barrier x1, local copies, waits for them, and re-layouts, on_device(): outcome = lax.optimization_barrier(outcome.astype(jnp.bfloat16))  21.2 us
  transfers between devices with their start and end apart: 2, of which 2 were waited for; matrix products, arithmetic and copies ran while one was open for 0% of the time, Pallas kernels for 0%

profile of v1, /device:TPU:2, one launch (start us, length us, event | category | flops | bytes accessed | tf_op | source)
XLA Modules:
  0.0 718.3 jit_solution(1712563968607605538)
XLA Ops:
  6.5 0.9 copy.34
  7.4 0.1 eq.65
  7.5 0.1 fusion.14
  7.6 0.2 reduce_window_sum.22
  7.8 0.2 select_reduce_fusion.1
  8.0 0.1 reduce_sum.32
  8.1 0.1 fusion.13
  8.2 2.7 convolution_convert_fusion.1
  10.9 4.1 reshape.233
  15.0 3.6 copy.36
  18.6 28.4 %all_to_all.35 = bf16[32,2,3,4096]{3,1,2,0:T(2,128)(2,1)S(1)} all-to-all(bf16[32,2,3,4096]{3,1,2,0:T(2,128)(2,1)S(1)} %copy.36), channel_id=1, replica_groups=mesh['rep'=8,'exp'=32] {'exp'}, dimensions={0} | all-to-all | bytes 3145728 | tf_op jit(solution)/shard_map/all_to_all | solution.py:48
  47.0 2.1 copy.37
  49.1 7.6 %stack.5 = bf16[8,1,2,96,4096]{4,3,2,1,0:T(8,128)(2,1)} broadcast(bf16[2,96,4096]{2,1,0:T(8,128)(2,1)} %copy.37), dimensions={2,3,4} | broadcast | bytes 14155776 | tf_op jit(solution)/shard_map/stack | solution.py:50
  56.7 285.3 %all_to_all.36 = bf16[8,1,2,96,4096]{4,3,2,1,0:T(8,128)(2,1)S(1)} all-to-all(bf16[8,1,2,96,4096]{4,3,2,1,0:T(8,128)(2,1)} %stack.5), channel_id=1, replica_groups=mesh['rep'=8,'exp'=32] {'rep'}, dimensions={0} | all-to-all | bytes 25165824 | tf_op jit(solution)/shard_map/all_to_all | solution.py:50
  341.9 5.1 copy.38
  347.1 10.8 %fusion.24 = f32[2,768,192]{1,2,0:T(8,128)} fusion(bf16[2,768,4096]{2,1,0:T(8,128)(2,1)} %bitcast.37, bf16[2,192,4096]{2,1,0:T(8,128)(2,1)} %param.9), kind=kOutput, calls=%fused_computation.44 | convolution fusion | flops 2415919104 | bytes 16908288 | tf_op jit(solution)/shard_map/emd,efd->emf/dot_general | solution.py:52
  357.9 15.9 %convolution_convert_fusion = bf16[2,768,4096]{2,1,0:T(8,128)(2,1)} fusion(bf16[2,192,4096]{2,1,0:T(8,128)(2,1)S(1)} %copy-done, bf16[2,768,4096]{2,1,0:T(8,128)(2,1)} %bitcast.38, bf16[2,192,4096]{2,1,0:T(8,128)(2,1)} %param.10, f32[2,768,192]{1,2,0:T(8,128)} %fusion.24), kind=kOutput, calls=%fused_computation.3 | convolution fusion | flops 4839899136 | bytes 32636928 | tf_op jit(solution)/shard_map/emf,efd->emd/dot_general | solution.py:57
  373.8 21.2 %copy.39 = bf16[2,768,4096]{2,0,1:T(2,128)(2,1)S(1)} copy(bf16[2,768,4096]{2,1,0:T(8,128)(2,1)} %convolution_convert_fusion) | data formatting | bytes 25165824 | tf_op jit(solution)/shard_map/optimization_barrier | solution.py:58
  395.1 11.5 %copy.40 = bf16[2,8,32,3,4096]{4,0,3,1,2:T(2,128)(2,1)} copy(bf16[2,8,32,3,4096]{4,0,3,2,1:T(2,128)(2,1)S(1)} %bitcast.36) | data formatting | bytes 25165824 | tf_op jit(solution)/shard_map/reshape;broadcast_in_dim | solution.py:60
  406.6 6.4 all-to-all-start.2
  413.1 24.7 %all-gather = f32[8,16,8]{1,2,0:T(8,128)S(1)} all-gather(f32[1,16,8]{1,2,0:T(8,128)S(1)} %convert_bitcast_fusion.1), channel_id=1, replica_groups=mesh['rep'=8,'exp'=32] {'rep'}, dimensions={0}, use_global_device_ids=true | all-gather | bytes 4608 | tf_op jit(solution)/shard_map/all_gather | solution.py:28
  437.8 0.1 copy.47
  437.9 2.5 select_reduce_fusion
  440.4 0.1 copy.42
  440.5 0.1 mul.56
  440.7 24.9 %all-gather.1 = f32[8,16,8]{1,2,0:T(8,128)S(1)} all-gather(f32[1,16,8]{1,2,0:T(8,128)S(1)} %bitcast.41), channel_id=1, replica_groups=mesh['rep'=8,'exp'=32] {'rep'}, dimensions={0}, use_global_device_ids=true | all-gather | bytes 4608 | tf_op jit(solution)/shard_map/all_gather | solution.py:27
  465.7 114.3 %all-to-all-done.2 = bf16[2,8,32,3,4096]{4,0,3,1,2:T(2,128)(2,1)} async-done(((bf16[2,8,32,3,4096]{4,0,3,1,2:T(2,128)(2,1)}), bf16[2,8,32,3,4096]{4,0,3,1,2:T(2,128)(2,1)}, u32[]{:S(2)}, u32[]{:S(2)}) %all-to-all-start.2) | async-done | bytes 12582944 | tf_op jit(solution)/shard_map/all_to_all | solution.py:65
  579.9 14.5 %copy.41 = bf16[32,2,8,1,3,4096]{5,2,4,1,0,3:T(8,128)(2,1)} copy(bf16[32,2,8,1,3,4096]{5,1,4,2,0,3:T(2,128)(2,1)} %bitcast.7) | data formatting | bytes 25165824 | tf_op jit(solution)/shard_map/all_to_all | solution.py:65
  594.4 34.4 %gather_fusion = bf16[1024,4096]{1,0:T(8,128)(2,1)} fusion(bf16[64,8,3,4096]{3,1,2,0:T(8,128)(2,1)} %bitcast.34, s32[1024]{0:T(1024)S(1)} %fusion.19), kind=kCustom, calls=%fused_computation | custom fusion | bytes 16789504 | tf_op jit(solution)/shard_map/gather | solution.py:72
  628.9 12.9 %fusion = f32[8,16,4096]{2,1,0:T(8,128)} fusion(f32[8,16,8]{2,1,0:T(8,128)S(1)} %copy.46, bf16[1024,4096]{1,0:T(8,128)(2,1)} %gather_fusion), kind=kLoop, calls=%fused_computation.2 | loop fusion | flops 12058624 | bytes 10489856 | tf_op jit(solution)/shard_map/reduce_sum | solution.py:74
  641.8 68.0 %reduce-scatter.2.cloned.1.call-done = f32[1,16,4096]{2,1,0:T(8,128)} async-done(((f32[8,16,4096]{2,1,0:T(8,128)}), f32[1,16,4096]{2,1,0:T(8,128)}) %reduce-scatter.2.cloned.1.call-update) | async-done | bytes 262160 | tf_op jit(solution)/shard_map/reduce_scatter | solution.py:79
  709.8 1.6 convert_bitcast_fusion
  (17 shorter events, 0.2 us)
Async XLA Ops:
  6.5 351.4 %copy-start = (bf16[2,192,4096]{2,1,0:T(8,128)(2,1)S(1)}, bf16[2,192,4096]{2,1,0:T(8,128)(2,1)}, u32[]{:S(2)}) copy-start(bf16[2,192,4096]{2,1,0:T(8,128)(2,1)} %param.11) | copy-start | bytes 9437188
  406.6 6.5 copy-start.2
  406.6 34.0 %copy-start.3 = (f32[16,8]{0,1:T(8,128)S(1)}, f32[16,8]{0,1:T(8,128)}, u32[]{:S(2)}) copy-start(f32[16,8]{0,1:T(8,128)} %param.8) | copy-start | bytes 1540
  406.6 173.3 %all-to-all-start.2 = ((bf16[2,8,32,3,4096]{4,0,3,1,2:T(2,128)(2,1)}), bf16[2,8,32,3,4096]{4,0,3,1,2:T(2,128)(2,1)}, u32[]{:S(2)}, u32[]{:S(2)}) async-start(bf16[2,8,32,3,4096]{4,0,3,1,2:T(2,128)(2,1)} %copy.40), calls=%async_computation.2 | async-start | bytes 25165824 | tf_op jit(solution)/shard_map/all_to_all | solution.py:65
  413.0 296.8 %reduce-scatter.2.cloned.1.call-start = ((), (), s32[]{:S(2)}) async-start(), calls=%async_computation.4 | async-start | bytes 2359296 | tf_op jit(solution)/shard_map/reduce_scatter | solution.py:79
  628.9 82.6 %copy-start.1 = (bf16[2,192,4096]{2,1,0:T(8,128)(2,1)S(1)}, bf16[2,192,4096]{2,1,0:T(8,128)(2,1)}, u32[]{:S(2)}) copy-start(bf16[2,192,4096]{2,1,0:T(8,128)(2,1)} %param.11) | copy-start | bytes 9437188
Sparse Core Ops, SparseCore 0:
  641.9 67.7 reduce-scatter.1
